TPU v7x, 32 devices: a whole 2x2x4 slice. The times are simulated.
32 devices in a mesh: row: 4 (over z), col: 8 (over y, x, core).
Axes of the slice: x: 2, y: 2, z: 4, core: 2. Of those that a mesh axis runs over, the one named last changes fastest.
Arguments:
- rhs_front: float32 [4, 6144, 1024], P(None, 'row', 'col'), may hold values from -6 to 6
- lower_blocks: float32 [6, 6144, 6144], P(None, 'row', 'col'), may hold values from -0.046875 to 0.046875
- panel_inverse: float32 [4, 6144, 6144], P(None, 'col', 'row'), may hold values from -0.078125 to 0.078125
- child_rows: float32 [4, 64, 128, 1024], P('row', 'col'), may hold values from -4 to 4
- child_map: int32 [4, 64], P('row', 'col'), may hold values from 0 to 47
- child_owner: int32 [8, 24, 1], P('col'), may hold values from 0 to 3; in each aligned block of 24 rows (0 to 23, 24 to 47, ..., all dimensions but the last counted through in order) at most 7 rows name the same one
Outputs:
- solution: float32 [4, 6144, 1024], P(None, 'col')
- child_rhs: float32 [8, 4, 7, 128, 1024], P('col', 'row')
Inputs may be any that keep to these rules, and one draw needn't show every extreme that they name: `child_map`: several child update blocks may name the same front block. `child_owner`: of the 24 solved blocks of one column group, at most 7 name the same row group, and in some column group one row group is named exactly 7 times.
All inputs are finite; a program needn't handle non-finite values.
Results may differ from a plain program's by a relative error of at most 0.00012.
Values sent between devices are 32-bit elements; how exact they have to be, the bound alone decides.
A program may use at most 192 MiB of HBM per device.

v0:
```python
import jax
import jax.numpy as jnp
from jax import lax
from jax.sharding import PartitionSpec as P


def on_device(rhs_front, lower_blocks, panel_inverse, child_rows, child_map, child_owner):
    highest = lax.Precision.HIGHEST
    row_count = lax.axis_size("row")
    row_at = lax.axis_index("row")
    col_at = lax.axis_index("col")
    panels, row_span, narrow = rhs_front.shape
    col_span = panel_inverse.shape[1]
    block = child_rows.shape[2]
    width = child_rows.shape[3]
    local_blocks = panels * row_span // block
    per_panel = col_span // block
    held_blocks = panels * per_panel
    most = max(2, held_blocks // row_count + 1)
    share = width // row_count
    targets = jnp.arange(local_blocks, dtype=jnp.int32)
    picks = (child_map[0][None, :] == targets[:, None]).astype(jnp.float32)
    added = jnp.einsum("lk,kbr->lbr", picks, child_rows[0], precision=highest).reshape(
        panels, row_span, width
    )
    placed = lax.dynamic_update_slice(
        jnp.zeros((panels, row_span, width), jnp.float32), rhs_front, (0, 0, col_at * narrow)
    )
    assembled = added + placed
    owner = child_owner[0, :, 0]
    hits = (owner[None, :] == jnp.arange(row_count, dtype=jnp.int32)[:, None]).astype(jnp.int32)
    ranks = jnp.cumsum(hits, axis=1) - hits
    slot_match = (ranks[:, None, :] == jnp.arange(most, dtype=jnp.int32)[None, :, None]).astype(
        jnp.int32
    )
    routing = (hits[:, None, :] * slot_match).astype(jnp.float32)
    solved = []
    for panel in range(panels):
        front = assembled[panel]
        for prior in range(panel):
            front = front - jnp.dot(
                lower_blocks[panel * (panel - 1) // 2 + prior],
                solved[prior],
                precision=highest,
                preferred_element_type=jnp.float32,
            )
        front = lax.psum(front, "col")
        partial_value = jnp.dot(
            panel_inverse[panel], front, precision=highest, preferred_element_type=jnp.float32
        )
        current = lax.psum(partial_value, "row")
        solved.append(current)
    solution = jnp.stack(solved)
    mine = lax.dynamic_slice_in_dim(
        solution.reshape(held_blocks, block, width), row_at * share, share, 2
    )
    sending = jnp.einsum("dsk,kbr->dsbr", routing, mine, precision=highest)
    received = lax.all_to_all(sending, "row", split_axis=0, concat_axis=3, tiled=True)
    return (solution, received.reshape(1, 1, most, block, width))


def solution(mesh):
    return jax.shard_map(
        on_device,
        mesh=mesh,
        in_specs=(
            P(None, "row", "col"),
            P(None, "row", "col"),
            P(None, "col", "row"),
            P("row", "col", None, None),
            P("row", "col"),
            P("col", None, None),
        ),
        out_specs=(P(None, "col", None), P("col", "row", None, None, None)),
        check_vma=False,
    )
```

profile of v0, /device:TPU:0, one launch (start us, length us, event | category | flops | bytes accessed | tf_op | source)
XLA Modules:
  0.0 1298.2 jit_solution(18290730721862400627)
XLA Ops:
  7.2 16.1 %fusion.38 = f32[48,128,1024]{2,0,1:T(8,128)S(1)} fusion(f32[8,128,1024]{2,1,0:T(8,128)} %bitcast.124, s32[8]{0:T(128)} %bitcast.129), kind=kOutput, calls=%fused_computation.41 | convolution fusion | flops 603980160 | bytes 29360160 | tf_op jit(solution)/shard_map/lk,kbr->lbr/dot_general | solution.py:23
  23.3 27.6 %copy.18 = f32[48,128,1024]{2,1,0:T(8,128)} copy(f32[48,128,1024]{2,0,1:T(8,128)S(1)} %fusion.38) | data formatting | bytes 50331648 | tf_op jit(solution)/shard_map/lk,kbr->lbr/dot_general | solution.py:23
  50.9 25.1 %copy.21 = f32[4,1536,1024]{1,2,0:T(8,128)} copy(f32[4,1536,1024]{2,1,0:T(8,128)} %bitcast.120) | data formatting | bytes 50331648 | tf_op jit(solution)/shard_map/reshape | solution.py:23
  88.5 106.8 %all-reduce.9.cloned.1.call-done = f32[1536,1024]{0,1:T(8,128)} async-done(((f32[1536,1024]{0,1:T(8,128)}), f32[1536,1024]{0,1:T(8,128)}) %all-reduce.9.cloned.1.call-update) | async-done | bytes 6291472 | tf_op jit(solution)/shard_map/psum | solution.py:47
  195.3 19.5 %fusion.45 = f32[768,1024]{0,1:T(8,128)} fusion(f32[1536,1024]{0,1:T(8,128)} %all-reduce.9.cloned.1.call-done, f32[4,768,1536]{2,1,0:T(8,128)} %param.8), kind=kOutput, calls=%fused_computation.46 | convolution fusion | flops 14495514624 | bytes 14155776 | tf_op jit(solution)/shard_map/dot_general | solution.py:48
  214.9 121.3 %all-reduce.11.cloned.1.call-done = f32[768,1024]{0,1:T(8,128)} async-done(((f32[768,1024]{0,1:T(8,128)}), f32[768,1024]{0,1:T(8,128)}) %all-reduce.11.cloned.1.call-update) | async-done | bytes 3145744 | tf_op jit(solution)/shard_map/psum | solution.py:51
  336.1 19.6 %fusion.5 = f32[1536,1024]{0,1:T(8,128)} fusion(f32[4,1536,1024]{1,2,0:T(8,128)} %add_dynamic-update-slice_fusion, f32[768,1024]{0,1:T(8,128)} %all-reduce.11.cloned.1.call-done, f32[6,1536,768]{2,1,0:T(8,128)} %param.7), kind=kOutput, calls=%fused_computation.9 | convolution fusion | flops 14497087488 | bytes 20447232 | tf_op jit(solution)/shard_map/dot_general | solution.py:41
  355.8 103.0 %all-reduce.13.cloned.1.call-done = f32[1536,1024]{0,1:T(8,128)} async-done(((f32[1536,1024]{0,1:T(8,128)}), f32[1536,1024]{0,1:T(8,128)}) %all-reduce.13.cloned.1.call-update) | async-done | bytes 6291472 | tf_op jit(solution)/shard_map/psum | solution.py:47
  458.9 19.6 %fusion.48 = f32[768,1024]{0,1:T(8,128)} fusion(f32[1536,1024]{0,1:T(8,128)} %all-reduce.13.cloned.1.call-done, f32[4,768,1536]{2,1,0:T(8,128)} %param.8), kind=kOutput, calls=%fused_computation.47 | convolution fusion | flops 14495514624 | bytes 14155776 | tf_op jit(solution)/shard_map/dot_general | solution.py:48
  478.6 121.3 %all-reduce.15.cloned.1.call-done = f32[768,1024]{0,1:T(8,128)} async-done(((f32[768,1024]{0,1:T(8,128)}), f32[768,1024]{0,1:T(8,128)}) %all-reduce.15.cloned.1.call-update) | async-done | bytes 3145744 | tf_op jit(solution)/shard_map/psum | solution.py:51
  599.8 18.3 %fusion.16 = f32[1024,1536]{1,0:T(8,128)S(1)} fusion(f32[768,1024]{0,1:T(8,128)} %all-reduce.15.cloned.1.call-done, f32[6,1536,768]{2,1,0:T(8,128)} %param.7), kind=kOutput, calls=%fused_computation.21 | convolution fusion | flops 14495514624 | bytes 14155776 | tf_op jit(solution)/shard_map/dot_general | solution.py:41
  618.1 19.5 %fusion.4 = f32[1536,1024]{0,1:T(8,128)} fusion(f32[4,1536,1024]{1,2,0:T(8,128)} %add_dynamic-update-slice_fusion, f32[1024,1536]{1,0:T(8,128)S(1)} %fusion.16, f32[768,1024]{0,1:T(8,128)S(1)} %copy-done, f32[6,1536,768]{2,1,0:T(8,128)} %param.7), kind=kOutput, calls=%fused_computation.7 | convolution fusion | flops 14498660352 | bytes 26738688 | tf_op jit(solution)/shard_map/dot_general | solution.py:41
  637.7 103.0 %all-reduce.17.cloned.1.call-done = f32[1536,1024]{0,1:T(8,128)} async-done(((f32[1536,1024]{0,1:T(8,128)}), f32[1536,1024]{0,1:T(8,128)}) %all-reduce.17.cloned.1.call-update) | async-done | bytes 6291472 | tf_op jit(solution)/shard_map/psum | solution.py:47
  740.7 19.5 %fusion.51 = f32[768,1024]{0,1:T(8,128)} fusion(f32[1536,1024]{0,1:T(8,128)} %all-reduce.17.cloned.1.call-done, f32[4,768,1536]{2,1,0:T(8,128)} %param.8), kind=kOutput, calls=%fused_computation.48 | convolution fusion | flops 14495514624 | bytes 14155776 | tf_op jit(solution)/shard_map/dot_general | solution.py:48
  760.3 20.1 %fusion.10 = f32[1024,1536]{1,0:T(8,128)} fusion(f32[768,1024]{0,1:T(8,128)} %all-reduce.15.cloned.1.call-done, f32[6,1536,768]{2,1,0:T(8,128)} %param.7), kind=kOutput, calls=%fused_computation.15 | convolution fusion | flops 14495514624 | bytes 14155776 | tf_op jit(solution)/shard_map/dot_general | solution.py:41
  780.4 101.2 %all-reduce.19.cloned.1.call-done = f32[768,1024]{0,1:T(8,128)} async-done(((f32[768,1024]{0,1:T(8,128)}), f32[768,1024]{0,1:T(8,128)}) %all-reduce.19.cloned.1.call-update) | async-done | bytes 3145744 | tf_op jit(solution)/shard_map/psum | solution.py:51
  881.6 18.8 %fusion.8 = f32[1024,1536]{1,0:T(8,128)S(1)} fusion(f32[768,1024]{0,1:T(8,128)} %all-reduce.19.cloned.1.call-done, f32[6,1536,768]{2,1,0:T(8,128)} %param.7), kind=kOutput, calls=%fused_computation.13 | convolution fusion | flops 14495514624 | bytes 14155776 | tf_op jit(solution)/shard_map/dot_general | solution.py:41
  900.4 19.7 %fusion.2 = f32[1536,1024]{0,1:T(8,128)} fusion(f32[4,1536,1024]{1,2,0:T(8,128)} %add_dynamic-update-slice_fusion, f32[1024,1536]{1,0:T(8,128)S(1)} %fusion.8, f32[1024,1536]{1,0:T(8,128)S(1)} %copy-done.1, f32[768,1024]{0,1:T(8,128)S(1)} %copy-done, f32[6,1536,768]{2,1,0:T(8,128)} %param.7), kind=kOutput, calls=%fused_computation.4 | convolution fusion | flops 14500233216 | bytes 33030144 | tf_op jit(solution)/shard_map/dot_general | solution.py:41
  920.2 103.0 %all-reduce.21.cloned.1.call-done = f32[1536,1024]{0,1:T(8,128)} async-done(((f32[1536,1024]{0,1:T(8,128)}), f32[1536,1024]{0,1:T(8,128)}) %all-reduce.21.cloned.1.call-update) | async-done | bytes 6291472 | tf_op jit(solution)/shard_map/psum | solution.py:47
  1023.2 19.7 %fusion.54 = f32[1,768,1024]{1,2,0:T(8,128)} fusion(f32[1536,1024]{0,1:T(8,128)} %all-reduce.21.cloned.1.call-done, f32[4,768,1536]{2,1,0:T(8,128)} %param.8), kind=kOutput, calls=%fused_computation.49 | convolution fusion | flops 14495514624 | bytes 14155776 | tf_op jit(solution)/shard_map/dot_general | solution.py:48
  1043.1 121.1 %all-reduce.23.cloned.1.call-done = f32[1,768,1024]{1,2,0:T(8,128)} async-done(((f32[1,768,1024]{1,2,0:T(8,128)}), f32[1,768,1024]{1,2,0:T(8,128)}) %all-reduce.23.cloned.1.call-update) | async-done | bytes 3145744 | tf_op jit(solution)/shard_map/psum | solution.py:51
  1164.2 9.1 pad_maximum_fusion
  1173.3 12.6 copy.26
  1196.0 85.4 %all_to_all.15 = f32[4,7,128,256]{3,2,1,0:T(8,128)} all-to-all(f32[4,7,128,256]{3,2,1,0:T(8,128)S(1)} %copy.24), channel_id=1, replica_groups=mesh['row'=4,'col'=8] {'row'}, dimensions={0} | all-to-all | bytes 7340032 | tf_op jit(solution)/shard_map/all_to_all | solution.py:58
  (33 shorter events, 32.8 us)
Async XLA Ops:
  7.2 188.1 %all-reduce.9.cloned.1.call-start = ((), (), s32[]{:S(2)}) async-start(), calls=%async_computation.1 | async-start | bytes 12582912 | tf_op jit(solution)/shard_map/psum | solution.py:47
  88.4 247.7 %all-reduce.11.cloned.1.call-start = ((), (), s32[]{:S(2)}) async-start(), calls=%async_computation.2 | async-start | bytes 6291456 | tf_op jit(solution)/shard_map/psum | solution.py:51
  214.8 244.0 %all-reduce.13.cloned.1.call-start = ((), (), s32[]{:S(2)}) async-start(), calls=%async_computation.3 | async-start | bytes 12582912 | tf_op jit(solution)/shard_map/psum | solution.py:47
  355.8 244.1 %all-reduce.15.cloned.1.call-start = ((), (), s32[]{:S(2)}) async-start(), calls=%async_computation.4 | async-start | bytes 6291456 | tf_op jit(solution)/shard_map/psum | solution.py:51
  478.5 139.6 %copy-start = (f32[768,1024]{0,1:T(8,128)S(1)}, f32[768,1024]{0,1:T(8,128)}, u32[]{:S(2)}) copy-start(f32[768,1024]{0,1:T(8,128)} %all-reduce.11.cloned.1.call-done) | copy-start | bytes 9437188
  478.5 262.2 %all-reduce.17.cloned.1.call-start = ((), (), s32[]{:S(2)}) async-start(), calls=%async_computation.5 | async-start | bytes 12582912 | tf_op jit(solution)/shard_map/psum | solution.py:47
  637.7 243.9 %all-reduce.19.cloned.1.call-start = ((), (), s32[]{:S(2)}) async-start(), calls=%async_computation.6 | async-start | bytes 6291456 | tf_op jit(solution)/shard_map/psum | solution.py:51
  760.3 262.9 %all-reduce.21.cloned.1.call-start = ((), (), s32[]{:S(2)}) async-start(), calls=%async_computation.7 | async-start | bytes 12582912 | tf_op jit(solution)/shard_map/psum | solution.py:47
  881.6 18.8 %copy-start.1 = (f32[1024,1536]{1,0:T(8,128)S(1)}, f32[1024,1536]{1,0:T(8,128)}, u32[]{:S(2)}) copy-start(f32[1024,1536]{1,0:T(8,128)} %fusion.10) | copy-start | bytes 18874372
  920.1 122.8 %copy-start.2 = (s32[1,24,1]{1,2,0:T(1,128)S(1)}, s32[1,24,1]{1,2,0:T(1,128)}, u32[]{:S(2)}) copy-start(s32[1,24,1]{1,2,0:T(1,128)} %param.11) | copy-start | bytes 292
  920.1 244.1 %all-reduce.23.cloned.1.call-start = ((), (), s32[]{:S(2)}) async-start(), calls=%async_computation.8 | async-start | bytes 6291456 | tf_op jit(solution)/shard_map/psum | solution.py:51
Sparse Core Ops, SparseCore 0:
  88.6 106.6 all-reduce.8
  214.9 121.1 all-reduce.10
  355.9 102.9 all-reduce.12
  478.6 121.1 all-reduce.14
  637.8 102.9 all-reduce.16
  760.4 121.1 all-reduce.18
  920.2 102.8 all-reduce.20
  1043.0 121.1 all-reduce.22
where the time goes:
time: 1310 us; the launch traced here: 1300 us
  waiting for transfers between devices  881 us (67%)
  matrix products  217 us (17%)
  local copies, waits for them, and re-layouts  86.5 us (7%)
  blocking collectives  85.4 us (7%)
  between operations  14.6 us (1%)
  other arithmetic  13.4 us (1%)
    psum x4, waiting for transfers between devices, on_device(): current = lax.psum(partial_value, 'row')  465 us
    psum x4, waiting for transfers between devices, on_device(): front = lax.psum(front, 'col')  416 us
    dot_general x6, matrix products, on_device(): jnp.dot(lower_blocks[panel * (panel - 1) // 2 + prior], solved[prior], pr...  116 us
    all_to_all x1, blocking collectives, on_device(): lax.all_to_all(sending, 'row', split_axis=0, concat_axis=3, tiled=True)  85.4 us
    dot_general x4, matrix products, on_device(): jnp.dot(panel_inverse[panel], front, precision=highest, preferred_element...  78.3 us
    dot_general x1, local copies, waits for them, and re-layouts, on_device(): jnp.einsum('lk,kbr->lbr', picks, child_rows[0], precision=highest)  27.6 us
  transfers between devices with their start and end apart: 8, of which 8 were waited for; matrix products, arithmetic and copies ran while one was open for 2% of the time, Pallas kernels for 0%

commit v1 on v0

--- a/solution.py
+++ b/solution.py
@@ -1,7 +1,40 @@
+import functools
 import jax
 import jax.numpy as jnp
 from jax import lax
 from jax.sharding import PartitionSpec as P
+
+
+def raise_arrays(block_in, in_dim, v0):
+    o_now = block_in.shape
+    b_next = block_in.reshape(*o_now[:in_dim], v0, o_now[in_dim] // v0, *o_now[in_dim + 1 :])
+    return jnp.moveaxis(b_next, in_dim, 0)
+
+
+def files_supply(own_rows, row_dim):
+    row_out = list(own_rows.shape[1:])
+    row_out[row_dim] *= own_rows.shape[0]
+    return jnp.moveaxis(own_rows, 0, row_dim).reshape(row_out)
+
+
+def assign_node(state, mesh_name, packet, row_data):
+    current_value, right_arr = (lax.psum(1, axis_name=mesh_name), lax.axis_index(mesh_name))
+    met_up = raise_arrays(state, packet, current_value)
+    no = 1
+    slots = [met_up[right_arr]]
+    while no < current_value:
+        block_last = met_up[right_arr ^ no]
+        slots.append(
+            lax.ppermute(
+                block_last, mesh_name, [(hop_no, hop_no ^ no) for hop_no in range(current_value)]
+            )
+        )
+        no += 1
+    met_up = jnp.stack(slots)[right_arr ^ jnp.arange(current_value)]
+    return files_supply(met_up, row_data)
+
+
+press_the_wires = functools.partial(assign_node, mesh_name="row", packet=0, row_data=3)
 
 
 def on_device(rhs_front, lower_blocks, panel_inverse, child_rows, child_map, child_owner):
@@ -55,7 +88,7 @@
         solution.reshape(held_blocks, block, width), row_at * share, share, 2
     )
     sending = jnp.einsum("dsk,kbr->dsbr", routing, mine, precision=highest)
-    received = lax.all_to_all(sending, "row", split_axis=0, concat_axis=3, tiled=True)
+    received = press_the_wires(sending)
     return (solution, received.reshape(1, 1, most, block, width))
 
 

time: 1310 us -> 1310 us (level); the launches traced: 1300 us -> 1280 us
  blocking collectives: 85.4 us -> 0 us
  waiting for transfers between devices: 881 us -> 939 us
    all_to_all x1 -> x0, blocking collectives: 85.4 us -> none  [on_device(): lax.all_to_all(sending, 'row', split_axis=0, concat_axis=3, tiled=True)]
    ppermute x0 -> x3, waiting for transfers between devices: none -> 58.4 us  [assign_node(): lax.ppermute(block_last, mesh_name, [(hop_no, hop_no ^ no) for hop_no in...]
  transfers between devices with their start and end apart: 8 -> 11, of which waited for: 8 -> 10; matrix products, arithmetic and copies ran while one was open for 2% -> 2% of each run, Pallas kernels for 0% -> 0%
where the time goes in v1:
time: 1310 us; the launch traced here: 1280 us
  waiting for transfers between devices  939 us (72%)
  matrix products  217 us (17%)
  local copies, waits for them, and re-layouts  91.6 us (7%)
  other arithmetic  15.6 us (1%)
  between operations  14.5 us (1%)
    psum x4, waiting for transfers between devices, on_device(): current = lax.psum(partial_value, 'row')  465 us
    psum x4, waiting for transfers between devices, on_device(): front = lax.psum(front, 'col')  416 us
    dot_general x6, matrix products, on_device(): jnp.dot(lower_blocks[panel * (panel - 1) // 2 + prior], solved[prior], pr...  116 us
    dot_general x4, matrix products, on_device(): jnp.dot(panel_inverse[panel], front, precision=highest, preferred_element...  78.1 us
    ppermute x3, waiting for transfers between devices, assign_node(): lax.ppermute(block_last, mesh_name, [(hop_no, hop_no ^ no) for hop_no in...  58.4 us
    dot_general x1, local copies, waits for them, and re-layouts, on_device(): jnp.einsum('lk,kbr->lbr', picks, child_rows[0], precision=highest)  27.5 us
  transfers between devices with their start and end apart: 11, of which 10 were waited for; matrix products, arithmetic and copies ran while one was open for 2% of the time, Pallas kernels for 0%

profile of v1, /device:TPU:0, one launch (start us, length us, event | category | flops | bytes accessed | tf_op | source)
XLA Modules:
  0.0 1283.0 jit_solution(12286293096081295869)
XLA Ops:
  7.2 16.1 %fusion.38 = f32[48,128,1024]{2,0,1:T(8,128)S(1)} fusion(f32[8,128,1024]{2,1,0:T(8,128)} %bitcast.133, s32[8]{0:T(128)} %bitcast.141), kind=kOutput, calls=%fused_computation.42 | convolution fusion | flops 603980160 | bytes 29360160 | tf_op jit(solution)/shard_map/lk,kbr->lbr/dot_general | solution.py:56
  23.3 27.5 %copy.30 = f32[48,128,1024]{2,1,0:T(8,128)} copy(f32[48,128,1024]{2,0,1:T(8,128)S(1)} %fusion.38) | data formatting | bytes 50331648 | tf_op jit(solution)/shard_map/lk,kbr->lbr/dot_general | solution.py:56
  50.8 25.1 %copy.33 = f32[4,1536,1024]{1,2,0:T(8,128)} copy(f32[4,1536,1024]{2,1,0:T(8,128)} %bitcast.128) | data formatting | bytes 50331648 | tf_op jit(solution)/shard_map/reshape | solution.py:56
  88.5 106.8 %all-reduce.9.cloned.1.call-done = f32[1536,1024]{0,1:T(8,128)} async-done(((f32[1536,1024]{0,1:T(8,128)}), f32[1536,1024]{0,1:T(8,128)}) %all-reduce.9.cloned.1.call-update) | async-done | bytes 6291472 | tf_op jit(solution)/shard_map/psum | solution.py:80
  195.2 19.5 %fusion.45 = f32[768,1024]{0,1:T(8,128)} fusion(f32[1536,1024]{0,1:T(8,128)} %all-reduce.9.cloned.1.call-done, f32[4,768,1536]{2,1,0:T(8,128)} %param.8), kind=kOutput, calls=%fused_computation.48 | convolution fusion | flops 14495514624 | bytes 14155776 | tf_op jit(solution)/shard_map/dot_general | solution.py:81
  214.8 121.3 %all-reduce.11.cloned.1.call-done = f32[768,1024]{0,1:T(8,128)} async-done(((f32[768,1024]{0,1:T(8,128)}), f32[768,1024]{0,1:T(8,128)}) %all-reduce.11.cloned.1.call-update) | async-done | bytes 3145744 | tf_op jit(solution)/shard_map/psum | solution.py:84
  336.1 19.6 %fusion.5 = f32[1536,1024]{0,1:T(8,128)} fusion(f32[4,1536,1024]{1,2,0:T(8,128)} %add_dynamic-update-slice_fusion, f32[768,1024]{0,1:T(8,128)} %all-reduce.11.cloned.1.call-done, f32[6,1536,768]{2,1,0:T(8,128)} %param.7), kind=kOutput, calls=%fused_computation.10 | convolution fusion | flops 14497087488 | bytes 20447232 | tf_op jit(solution)/shard_map/dot_general | solution.py:74
  355.8 103.0 %all-reduce.13.cloned.1.call-done = f32[1536,1024]{0,1:T(8,128)} async-done(((f32[1536,1024]{0,1:T(8,128)}), f32[1536,1024]{0,1:T(8,128)}) %all-reduce.13.cloned.1.call-update) | async-done | bytes 6291472 | tf_op jit(solution)/shard_map/psum | solution.py:80
  458.8 19.6 %fusion.48 = f32[768,1024]{0,1:T(8,128)} fusion(f32[1536,1024]{0,1:T(8,128)} %all-reduce.13.cloned.1.call-done, f32[4,768,1536]{2,1,0:T(8,128)} %param.8), kind=kOutput, calls=%fused_computation.49 | convolution fusion | flops 14495514624 | bytes 14155776 | tf_op jit(solution)/shard_map/dot_general | solution.py:81
  478.5 121.2 %all-reduce.15.cloned.1.call-done = f32[768,1024]{0,1:T(8,128)} async-done(((f32[768,1024]{0,1:T(8,128)}), f32[768,1024]{0,1:T(8,128)}) %all-reduce.15.cloned.1.call-update) | async-done | bytes 3145744 | tf_op jit(solution)/shard_map/psum | solution.py:84
  599.8 18.3 %fusion.16 = f32[1024,1536]{1,0:T(8,128)S(1)} fusion(f32[768,1024]{0,1:T(8,128)} %all-reduce.15.cloned.1.call-done, f32[6,1536,768]{2,1,0:T(8,128)} %param.7), kind=kOutput, calls=%fused_computation.22 | convolution fusion | flops 14495514624 | bytes 14155776 | tf_op jit(solution)/shard_map/dot_general | solution.py:74
  618.0 19.5 %fusion.4 = f32[1536,1024]{0,1:T(8,128)} fusion(f32[4,1536,1024]{1,2,0:T(8,128)} %add_dynamic-update-slice_fusion, f32[1024,1536]{1,0:T(8,128)S(1)} %fusion.16, f32[768,1024]{0,1:T(8,128)S(1)} %copy-done, f32[6,1536,768]{2,1,0:T(8,128)} %param.7), kind=kOutput, calls=%fused_computation.8 | convolution fusion | flops 14498660352 | bytes 26738688 | tf_op jit(solution)/shard_map/dot_general | solution.py:74
  637.6 103.0 %all-reduce.17.cloned.1.call-done = f32[1536,1024]{0,1:T(8,128)} async-done(((f32[1536,1024]{0,1:T(8,128)}), f32[1536,1024]{0,1:T(8,128)}) %all-reduce.17.cloned.1.call-update) | async-done | bytes 6291472 | tf_op jit(solution)/shard_map/psum | solution.py:80
  740.7 19.5 %fusion.51 = f32[768,1024]{0,1:T(8,128)} fusion(f32[1536,1024]{0,1:T(8,128)} %all-reduce.17.cloned.1.call-done, f32[4,768,1536]{2,1,0:T(8,128)} %param.8), kind=kOutput, calls=%fused_computation.50 | convolution fusion | flops 14495514624 | bytes 14155776 | tf_op jit(solution)/shard_map/dot_general | solution.py:81
  760.2 20.0 %fusion.10 = f32[1024,1536]{1,0:T(8,128)} fusion(f32[768,1024]{0,1:T(8,128)} %all-reduce.15.cloned.1.call-done, f32[6,1536,768]{2,1,0:T(8,128)} %param.7), kind=kOutput, calls=%fused_computation.16 | convolution fusion | flops 14495514624 | bytes 14155776 | tf_op jit(solution)/shard_map/dot_general | solution.py:74
  780.2 101.3 %all-reduce.19.cloned.1.call-done = f32[768,1024]{0,1:T(8,128)} async-done(((f32[768,1024]{0,1:T(8,128)}), f32[768,1024]{0,1:T(8,128)}) %all-reduce.19.cloned.1.call-update) | async-done | bytes 3145744 | tf_op jit(solution)/shard_map/psum | solution.py:84
  881.5 19.2 %fusion.8 = f32[1024,1536]{1,0:T(8,128)S(1)} fusion(f32[768,1024]{0,1:T(8,128)} %all-reduce.19.cloned.1.call-done, f32[6,1536,768]{2,1,0:T(8,128)} %param.7), kind=kOutput, calls=%fused_computation.14 | convolution fusion | flops 14495514624 | bytes 14155776 | tf_op jit(solution)/shard_map/dot_general | solution.py:74
  900.7 19.9 %fusion.2 = f32[1536,1024]{0,1:T(8,128)} fusion(f32[4,1536,1024]{1,2,0:T(8,128)} %add_dynamic-update-slice_fusion, f32[1024,1536]{1,0:T(8,128)S(1)} %fusion.8, f32[1024,1536]{1,0:T(8,128)S(1)} %copy-done.1, f32[768,1024]{0,1:T(8,128)S(1)} %copy-done, f32[6,1536,768]{2,1,0:T(8,128)} %param.7), kind=kOutput, calls=%fused_computation.5 | convolution fusion | flops 14500233216 | bytes 33030144 | tf_op jit(solution)/shard_map/dot_general | solution.py:74
  920.6 103.0 %all-reduce.21.cloned.1.call-done = f32[1536,1024]{0,1:T(8,128)} async-done(((f32[1536,1024]{0,1:T(8,128)}), f32[1536,1024]{0,1:T(8,128)}) %all-reduce.21.cloned.1.call-update) | async-done | bytes 6291472 | tf_op jit(solution)/shard_map/psum | solution.py:80
  1023.6 19.5 %fusion.54 = f32[1,768,1024]{1,2,0:T(8,128)} fusion(f32[1536,1024]{0,1:T(8,128)} %all-reduce.21.cloned.1.call-done, f32[4,768,1536]{2,1,0:T(8,128)} %param.8), kind=kOutput, calls=%fused_computation.51 | convolution fusion | flops 14495514624 | bytes 14155776 | tf_op jit(solution)/shard_map/dot_general | solution.py:81
  1043.4 121.1 %all-reduce.23.cloned.1.call-done = f32[1,768,1024]{1,2,0:T(8,128)} async-done(((f32[1,768,1024]{1,2,0:T(8,128)}), f32[1,768,1024]{1,2,0:T(8,128)}) %all-reduce.23.cloned.1.call-update) | async-done | bytes 3145744 | tf_op jit(solution)/shard_map/psum | solution.py:84
  1173.6 12.8 copy.42
  1201.2 35.3 %collective-permute-done = f32[1,7,128,256]{3,2,1,0:T(8,128)S(1)} collective-permute-done((f32[1,7,128,256]{3,2,1,0:T(8,128)S(1)}, f32[1,7,128,256]{3,2,1,0:T(8,128)S(1)}, u32[]{:S(2)}, u32[]{:S(2)}) %collective-permute-start) | collective-permute-done | bytes 917536 | tf_op jit(solution)/shard_map/ppermute | solution.py:28
  1236.6 23.1 %collective-permute-done.1 = f32[1,7,128,256]{3,2,1,0:T(8,128)S(1)} collective-permute-done((f32[1,7,128,256]{3,2,1,0:T(8,128)S(1)}, f32[1,7,128,256]{3,2,1,0:T(8,128)S(1)}, u32[]{:S(2)}, u32[]{:S(2)}) %collective-permute-start.1) | collective-permute-done | bytes 917536 | tf_op jit(solution)/shard_map/ppermute | solution.py:28
  (46 shorter events, 53.3 us)
Async XLA Ops:
  7.2 188.1 %all-reduce.9.cloned.1.call-start = ((), (), s32[]{:S(2)}) async-start(), calls=%async_computation | async-start | bytes 12582912 | tf_op jit(solution)/shard_map/psum | solution.py:80
  88.4 247.6 %all-reduce.11.cloned.1.call-start = ((), (), s32[]{:S(2)}) async-start(), calls=%async_computation.1 | async-start | bytes 6291456 | tf_op jit(solution)/shard_map/psum | solution.py:84
  214.8 244.0 %all-reduce.13.cloned.1.call-start = ((), (), s32[]{:S(2)}) async-start(), calls=%async_computation.2 | async-start | bytes 12582912 | tf_op jit(solution)/shard_map/psum | solution.py:80
  355.7 244.0 %all-reduce.15.cloned.1.call-start = ((), (), s32[]{:S(2)}) async-start(), calls=%async_computation.3 | async-start | bytes 6291456 | tf_op jit(solution)/shard_map/psum | solution.py:84
  478.4 139.6 %copy-start = (f32[768,1024]{0,1:T(8,128)S(1)}, f32[768,1024]{0,1:T(8,128)}, u32[]{:S(2)}) copy-start(f32[768,1024]{0,1:T(8,128)} %all-reduce.11.cloned.1.call-done) | copy-start | bytes 9437188
  478.5 262.2 %all-reduce.17.cloned.1.call-start = ((), (), s32[]{:S(2)}) async-start(), calls=%async_computation.4 | async-start | bytes 12582912 | tf_op jit(solution)/shard_map/psum | solution.py:80
  637.6 243.9 %all-reduce.19.cloned.1.call-start = ((), (), s32[]{:S(2)}) async-start(), calls=%async_computation.5 | async-start | bytes 6291456 | tf_op jit(solution)/shard_map/psum | solution.py:84
  760.2 263.5 %all-reduce.21.cloned.1.call-start = ((), (), s32[]{:S(2)}) async-start(), calls=%async_computation.6 | async-start | bytes 12582912 | tf_op jit(solution)/shard_map/psum | solution.py:80
  881.5 19.2 %copy-start.1 = (f32[1024,1536]{1,0:T(8,128)S(1)}, f32[1024,1536]{1,0:T(8,128)}, u32[]{:S(2)}) copy-start(f32[1024,1536]{1,0:T(8,128)} %fusion.10) | copy-start | bytes 18874372
  920.6 122.6 %copy-start.2 = (s32[1,24,1]{1,2,0:T(1,128)S(1)}, s32[1,24,1]{1,2,0:T(1,128)}, u32[]{:S(2)}) copy-start(s32[1,24,1]{1,2,0:T(1,128)} %param.11) | copy-start | bytes 292
  920.6 243.9 %all-reduce.23.cloned.1.call-start = ((), (), s32[]{:S(2)}) async-start(), calls=%async_computation.7 | async-start | bytes 6291456 | tf_op jit(solution)/shard_map/psum | solution.py:84
  1195.7 40.8 %collective-permute-start = (f32[1,7,128,256]{3,2,1,0:T(8,128)S(1)}, f32[1,7,128,256]{3,2,1,0:T(8,128)S(1)}, u32[]{:S(2)}, u32[]{:S(2)}) collective-permute-start(f32[1,7,128,256]{3,2,1,0:T(8,128)S(1)} %copy.37), channel_id=1, source_target_pairs={{0,8},{8,0},{16,24},{24,16},{1,9},{9,1},{17,25},{25,17},{2,10},{10... | collective-permute-start | bytes 2752520 | tf_op jit(solution)/shard_map/ppermute | solution.py:28
  1196.1 63.5 %collective-permute-start.1 = (f32[1,7,128,256]{3,2,1,0:T(8,128)S(1)}, f32[1,7,128,256]{3,2,1,0:T(8,128)S(1)}, u32[]{:S(2)}, u32[]{:S(2)}) collective-permute-start(f32[1,7,128,256]{3,2,1,0:T(8,128)S(1)} %copy.38), channel_id=1, source_target_pairs={{0,16},{8,24},{16,0},{24,8},{1,17},{9,25},{17,1},{25,9},{2,18},{10... | collective-permute-start | bytes 2752520 | tf_op jit(solution)/shard_map/ppermute | solution.py:28
  1198.1 61.5 %collective-permute-start.2 = (f32[1,7,128,256]{3,2,1,0:T(8,128)S(1)}, f32[1,7,128,256]{3,2,1,0:T(8,128)S(1)}, u32[]{:S(2)}, u32[]{:S(2)}) collective-permute-start(f32[1,7,128,256]{3,2,1,0:T(8,128)S(1)} %copy.39), channel_id=1, source_target_pairs={{0,24},{8,16},{16,8},{24,0},{1,25},{9,17},{17,9},{25,1},{2,26},{10... | collective-permute-start | bytes 2752520 | tf_op jit(solution)/shard_map/ppermute | solution.py:28
Sparse Core Ops, SparseCore 0:
  88.6 106.6 all-reduce.8
  214.9 121.1 all-reduce.10
  355.8 102.8 all-reduce.12
  478.6 121.1 all-reduce.14
  637.7 102.9 all-reduce.16
  760.3 121.1 all-reduce.18
  920.7 102.9 all-reduce.20
  1043.3 121.1 all-reduce.22
